TPU v7x, 512 devices: a whole 4x8x8 slice. The times are simulated.
512 devices in a mesh: grp: 16 (over y, x_hi), blk: 32 (over x_lo, z, core).
Axes of the slice: x: 4 (x_hi: 2, x_lo: 2; x = x_hi * 2 + x_lo), y: 8, z: 8, core: 2. Of those that a mesh axis runs over, the one named last changes fastest.
Arguments:
- sigma_anc: float32 [16384, 16384], P('grp', 'blk')
- panels: float32 [16384, 1024], P(('grp', 'blk')), may hold values from -0.0625 to 0.0625
- diag_inv: float32 [1024, 256], replicated, may hold values from -6 to 6
- scaled_parent_panel: float32 [512, 256], replicated, may hold values from -0.375 to 0.375
- struct_upper: int32 [2, 32], replicated, may hold values from 0 to 63, as said below
- struct_lower: int32 [2, 16], replicated, may hold values from 0 to 63, as said below
Outputs:
- cov_panel: float32 [16384, 1024], P(('blk', 'grp'))
- cov_diag: float32 [1024, 256], P('blk')
- cov_parent: float32 [512, 256], P('blk')
Inputs may be any that keep to these rules, and one draw needn't show every extreme that they name: `struct_upper`: each row lists 32 different ancestor blocks. `struct_lower`: each row lists 16 different blocks, all in its parent's row of struct_upper.
All inputs are finite; a program needn't handle non-finite values.
Results may differ from a plain program's by a relative error of at most 0.00011.
Values sent between devices are 32-bit elements; how exact they have to be, the bound alone decides.
A program may use at most 64 MiB of HBM per device.

v0:
```python
import jax
import jax.numpy as jnp
from jax import lax
from jax.sharding import PartitionSpec as P

NODE_WIDTH = 256
UPPER_NODES_1 = 2
LOWER_NODES_2 = 2


HIGH_ACCURACY = lax.Precision.HIGHEST


def block_table(struct_upper, struct_lower, blocks):
    ids = jnp.arange(blocks, dtype=jnp.int32)
    upper = jnp.any(struct_upper[:, :, None] == ids[None, None, :], axis=1)
    lower = jnp.any(struct_lower[:, :, None] == ids[None, None, :], axis=1)
    return jnp.concatenate([upper, lower], axis=0).astype(jnp.float32)


def row_mask(table, first_row, count):
    blocks = table.shape[1]
    rows = first_row + jnp.arange(count, dtype=jnp.int32)
    membership_grid = (
        (rows // NODE_WIDTH)[:, None] == jnp.arange(blocks, dtype=jnp.int32)[None, :]
    ).astype(jnp.float32)
    return jnp.dot(
        membership_grid, table.T, precision=HIGH_ACCURACY, preferred_element_type=jnp.float32
    )


def strip_summands(reciprocal_lines, array_lines, membership_grid, stacked_arrays):
    count = reciprocal_lines.shape[0]
    upper_width_1 = UPPER_NODES_1 * NODE_WIDTH
    matrix_columns = jnp.repeat(array_lines, NODE_WIDTH, axis=1)
    g_up = -(matrix_columns[:, :upper_width_1] * reciprocal_lines[:, :upper_width_1])
    collected_elder_share = jnp.einsum(
        "rjw,cj->rcw",
        g_up.reshape(count, UPPER_NODES_1, NODE_WIDTH),
        membership_grid,
        precision=HIGH_ACCURACY,
    )
    resolved_bottom_share = matrix_columns[:, upper_width_1:].reshape(
        count, LOWER_NODES_2, NODE_WIDTH
    ) * (
        jnp.einsum("odf,dfy->ody", collected_elder_share, stacked_arrays, precision=HIGH_ACCURACY)
        + reciprocal_lines[:, upper_width_1:].reshape(count, LOWER_NODES_2, NODE_WIDTH)
    )
    strip_result = jnp.concatenate(
        [g_up, -resolved_bottom_share.reshape(count, LOWER_NODES_2 * NODE_WIDTH)], axis=1
    )
    return (strip_result, collected_elder_share, resolved_bottom_share)


def block_sums(urows, reciprocal_lines, collected_elder_share, resolved_bottom_share):
    count = urows.shape[0]
    upper_width_1 = UPPER_NODES_1 * NODE_WIDTH
    u_up = urows[:, :upper_width_1].reshape(count, UPPER_NODES_1, NODE_WIDTH)
    u_low = urows[:, upper_width_1:].reshape(count, LOWER_NODES_2, NODE_WIDTH)
    amat = jnp.einsum(
        "rjw,rjv->jwv",
        u_up,
        reciprocal_lines[:, :upper_width_1].reshape(count, UPPER_NODES_1, NODE_WIDTH),
        precision=HIGH_ACCURACY,
    )
    block_matrix = jnp.einsum("rcw,rcv->cwv", u_low, collected_elder_share, precision=HIGH_ACCURACY)
    extra_matrix = jnp.einsum("rcw,rcv->cwv", u_low, resolved_bottom_share, precision=HIGH_ACCURACY)
    return jnp.concatenate([amat, block_matrix, extra_matrix], axis=0)


def per_device(sigma_anc, panels, diag_inv, scaled_parent_panel, struct_upper, struct_lower):
    rows_grp, cols_dev = sigma_anc.shape
    rows_dev = panels.shape[0]
    grp_count = lax.axis_size("grp")
    blk_count = lax.axis_size("blk")
    grp_pos = lax.axis_index("grp")
    blk_pos = lax.axis_index("blk")
    blocks = cols_dev * blk_count // NODE_WIDTH
    table = block_table(struct_upper, struct_lower, blocks)
    parent_ids = jnp.arange(LOWER_NODES_2, dtype=jnp.int32) % UPPER_NODES_1
    membership_grid = (
        parent_ids[:, None] == jnp.arange(UPPER_NODES_1, dtype=jnp.int32)[None, :]
    ).astype(jnp.float32)
    stacked_arrays = scaled_parent_panel.reshape(LOWER_NODES_2, NODE_WIDTH, NODE_WIDTH)
    first_in = grp_pos * rows_grp + blk_pos * rows_dev
    upanel = panels * jnp.repeat(row_mask(table, first_in, rows_dev), NODE_WIDTH, axis=1)
    grouped = lax.all_gather(upanel, "blk", axis=0, tiled=True)
    partial_value = lax.dot_general(
        sigma_anc,
        grouped,
        (((0,), (0,)), ((), ())),
        precision=HIGH_ACCURACY,
        preferred_element_type=jnp.float32,
    )
    share = cols_dev // grp_count
    col_first = blk_pos * cols_dev
    root = col_first // rows_grp
    offset = jnp.clip(col_first - grp_pos * rows_grp, 0, rows_grp - cols_dev)
    own_first = col_first + grp_pos * share
    owned_mask = row_mask(table, own_first, share)
    nterms = UPPER_NODES_1 + 2 * LOWER_NODES_2
    inverse_columns = lax.psum(partial_value, "grp")
    inverse_owned = lax.dynamic_slice_in_dim(inverse_columns, grp_pos * share, share, 0)
    strip_result, collected_elder_share, resolved_bottom_share = strip_summands(
        inverse_owned, owned_mask, membership_grid, stacked_arrays
    )

    def on_root():
        u_cols = lax.dynamic_slice_in_dim(grouped, offset, cols_dev, 0)
        complete_mask = row_mask(table, col_first, cols_dev)
        discarded_result, collected_entire_factor, resolved_entire_factor = strip_summands(
            inverse_columns, complete_mask, membership_grid, stacked_arrays
        )
        return block_sums(u_cols, inverse_columns, collected_entire_factor, resolved_entire_factor)

    def off_root():
        return jnp.zeros((nterms, NODE_WIDTH, NODE_WIDTH), jnp.float32)

    terms = lax.cond(grp_pos == root, on_root, off_root)
    summed = lax.psum(terms, ("grp", "blk"))
    amat = summed[:UPPER_NODES_1]
    block_matrix = summed[UPPER_NODES_1 : UPPER_NODES_1 + LOWER_NODES_2]
    extra_matrix = summed[UPPER_NODES_1 + LOWER_NODES_2 :]
    diagonal_matrices = diag_inv.reshape(UPPER_NODES_1 + LOWER_NODES_2, NODE_WIDTH, NODE_WIDTH)
    s_up = diagonal_matrices[:UPPER_NODES_1] + amat
    parent_selection = jnp.einsum("cj,jwv->cwv", membership_grid, s_up, precision=HIGH_ACCURACY)
    solved_parent = jnp.einsum(
        "ghz,gzs->ghs", parent_selection, stacked_arrays, precision=HIGH_ACCURACY
    ) + jnp.transpose(block_matrix, (0, 2, 1))
    lower_selection = (
        diagonal_matrices[UPPER_NODES_1:]
        + jnp.einsum("lmt,lmx->ltx", stacked_arrays, solved_parent, precision=HIGH_ACCURACY)
        + extra_matrix
    )
    whole_diag = jnp.concatenate([s_up, lower_selection], axis=0).reshape(
        (UPPER_NODES_1 + LOWER_NODES_2) * NODE_WIDTH, NODE_WIDTH
    )
    whole_parent = -solved_parent.reshape(LOWER_NODES_2 * NODE_WIDTH, NODE_WIDTH)
    diag_rows = (UPPER_NODES_1 + LOWER_NODES_2) * NODE_WIDTH // blk_count
    parent_rows = LOWER_NODES_2 * NODE_WIDTH // blk_count
    cov_diag = lax.dynamic_slice_in_dim(whole_diag, blk_pos * diag_rows, diag_rows, 0)
    cov_parent = lax.dynamic_slice_in_dim(whole_parent, blk_pos * parent_rows, parent_rows, 0)
    return (strip_result, cov_diag, cov_parent)


def solution(mesh):
    return jax.shard_map(
        per_device,
        mesh=mesh,
        in_specs=(P("grp", "blk"), P(("grp", "blk"), None), P(), P(), P(), P()),
        out_specs=(P(("blk", "grp"), None), P("blk", None), P("blk", None)),
        check_vma=False,
    )
```

profile of v0, /device:TPU:1, one launch (start us, length us, event | category | flops | bytes accessed | tf_op | source)
XLA Modules:
  0.0 598.4 jit_solution(4750005704873806624)
XLA Ops:
  9.3 1.6 mul.37
  10.9 75.6 %all-gather.2.cloned.1.call-done = f32[1024,1024]{1,0:T(8,128)} async-done(((f32[32,1024]{1,0:T(8,128)}), f32[1024,1024]{1,0:T(8,128)}) %all-gather.2.cloned.1.call-update) | async-done | bytes 4194320 | tf_op jit(solution)/shard_map/all_gather | solution.py:87
  86.5 9.6 %convolution_bitcast_fusion.2 = f32[512,1024]{0,1:T(8,128)} fusion(f32[1024,1024]{1,0:T(8,128)} %all-gather.2.cloned.1.call-done, f32[1024,512]{1,0:T(8,128)S(1)} %copy-done), kind=kOutput, calls=%fused_computation.24 | convolution fusion | flops 6442450944 | bytes 8388608 | tf_op jit(solution)/shard_map/dot_general | solution.py:88
  96.3 1.0 copy-done.8
  97.4 1.1 fusion.35
  98.5 159.0 %all-reduce.3.cloned.1.call-done = f32[512,1024]{0,1:T(8,128)} async-done(((f32[512,1024]{0,1:T(8,128)}), f32[512,1024]{0,1:T(8,128)}) %all-reduce.3.cloned.1.call-update) | async-done | bytes 2097168 | tf_op jit(solution)/shard_map/psum | solution.py:102
  257.4 31.1 %conditional.1 = (f32[6,256,256]{2,1,0:T(8,128)}) conditional(s32[]{:T(128)} %convert_element_type.12, () %tuple.14, (s32[]{:T(128)}, s32[]{:T(128)}, f32[1024,1024]{1,0:T(8,128)}, f32[512,1024]{0,1:T(8,128)}, f32[4,64]{1,0:T(4,128)S(1)}, /*index=5*/f32[2,2]{1,0:T(2,128)S(1)}, f32[2,256,256]{2,1,0:T(8,128)}) %tuple.39), branch_computations={%region_3.4_spmd, %region_4.5_spmd} | conditional | flops 3230965760 | bytes 63984808 | solution.py:119
  259.0 1.9 fusion.34
  260.9 1.3 copy.80
  262.2 4.9 convolution_bitcast_fusion
  267.1 2.6 copy.83
  269.7 2.6 copy.84
  272.3 3.8 fusion.1
  276.1 5.4 copy.92
  281.5 2.2 constant_dynamic-slice_fusion
  283.7 1.1 fusion.38
  284.9 1.1 fusion.4
  286.0 1.2 fusion.37
  287.2 1.3 pad_maximum_fusion
  288.5 3.1 copy.93
  291.8 1.0 copy.94
  292.8 1.0 copy.99
  293.9 1.3 fusion.19
  297.0 281.2 %all-reduce.5.cloned.1.call-done = f32[6,256,256]{1,2,0:T(8,128)} async-done(((f32[6,256,256]{1,2,0:T(8,128)}), f32[6,256,256]{1,2,0:T(8,128)}) %all-reduce.5.cloned.1.call-update) | async-done | bytes 1572880 | tf_op jit(solution)/shard_map/psum | solution.py:120
  578.2 1.3 slice_add_fusion
  579.5 1.0 copy.95
  580.5 2.2 fusion.27
  582.7 2.5 fusion.36
  585.2 2.1 fusion.13
  587.3 1.0 pad_maximum_fusion.1
  588.3 1.6 copy.100
  590.5 1.3 constant_dynamic-slice_fusion.1
  (47 shorter events, 6.6 us)
Async XLA Ops:
  7.2 79.4 %copy-start = (f32[1024,512]{1,0:T(8,128)S(1)}, f32[1024,512]{1,0:T(8,128)}, u32[]{:S(2)}) copy-start(f32[1024,512]{1,0:T(8,128)} %param.8) | copy-start | bytes 6291460
  7.2 79.3 %all-gather.2.cloned.1.call-start = ((), (), s32[]{:S(2)}) async-start(), calls=%async_computation | async-start | bytes 4325376 | tf_op jit(solution)/shard_map/all_gather | solution.py:87
  10.9 246.6 %all-reduce.3.cloned.1.call-start = ((), (), s32[]{:S(2)}) async-start(), calls=%async_computation.1 | async-start | bytes 4194304 | tf_op jit(solution)/shard_map/psum | solution.py:102
  96.1 1.2 copy-start.8
  96.2 482.0 %all-reduce.5.cloned.1.call-start = ((), (), s32[]{:S(2)}) async-start(), calls=%async_computation.2 | async-start | bytes 3145728 | tf_op jit(solution)/shard_map/psum | solution.py:120
  257.4 1.6 copy-start.4
  281.5 2.2 copy-start.2
  283.7 2.3 copy-start.3
  288.5 3.3 copy-start.7
  291.6 1.2 copy-start.6
  293.8 2.1 copy-start.1
  580.5 4.7 copy-start.5
Sparse Core Ops, SparseCore 0:
  11.0 75.4 all-gather.1
  96.3 161.1 all-reduce.2
  291.7 286.4 all-reduce.4
where the time goes:
time: 599 us; the launch traced here: 598 us
  waiting for transfers between devices  516 us (86%)
  matrix products  30 us (5%)
  local copies, waits for them, and re-layouts  27.6 us (5%)
  between operations  13.9 us (2%)
  other arithmetic  10.8 us (2%)
    psum x1, waiting for transfers between devices, per_device(): summed = lax.psum(terms, ('grp', 'blk'))  281 us
    psum x1, waiting for transfers between devices, per_device(): inverse_columns = lax.psum(partial_value, 'grp')  159 us
    all_gather x1, waiting for transfers between devices, per_device(): grouped = lax.all_gather(upanel, 'blk', axis=0, tiled=True)  75.6 us
  transfers between devices with their start and end apart: 3, of which 3 were waited for; matrix products, arithmetic and copies ran while one was open for 1% of the time, Pallas kernels for 0%

commit v1 on v0

v1 whole, which is shorter than its diff:
```python
import jax
import jax.numpy as jnp
from jax import lax
from jax.sharding import PartitionSpec as P

W = 256
HIGH = lax.Precision.HIGH
HIGHEST = lax.Precision.HIGHEST


def dot(a, b, ca, cb, precision=HIGH):
    return lax.dot_general(
        a, b, (((ca,), (cb,)), ((), ())), precision=precision, preferred_element_type=jnp.float32
    )


def listed(struct_upper, struct_lower, block):
    upper = jnp.any(struct_upper == block, axis=1)
    lower = jnp.any(struct_lower == block, axis=1)
    flags = jnp.concatenate([upper, lower]).astype(jnp.float32)
    return jnp.repeat(flags, W)[None, :]


def gather_rows(rows):
    return lax.all_gather(rows, "blk", axis=0, tiled=True)


def scatter_products(partial):
    return lax.psum_scatter(partial, "grp", scatter_dimension=0, tiled=True)


def sum_blocks(terms):
    return lax.psum(lax.psum_scatter(terms, "blk", scatter_dimension=0, tiled=True), "grp")


def per_device(sigma_anc, panels, diag_inv, scaled_parent_panel, struct_upper, struct_lower):
    grp = lax.axis_index("grp")
    blk = lax.axis_index("blk")
    v = [scaled_parent_panel[:W], scaled_parent_panel[W:]]
    u = panels * listed(struct_upper, struct_lower, (grp * 32 + blk) // 8)
    x = [dot(u[:, c * W : (c + 1) * W], v[c], 1, 0) - u[:, (c + 2) * W : (c + 3) * W] for c in (0, 1)]
    w = jnp.concatenate([u[:, : 2 * W], x[0], x[1]], axis=1)
    moves = [(q, (q % 16) * 32 + q // 16) for q in range(512)]
    w_own = lax.ppermute(w, ("grp", "blk"), moves)
    gathered = gather_rows(w)
    t = scatter_products(dot(sigma_anc, gathered, 0, 0))
    own = listed(struct_upper, struct_lower, (blk * 16 + grp) // 8)
    sign = jnp.where(jnp.arange(4 * W) < 2 * W, -1.0, 1.0).astype(jnp.float32)[None, :]
    cov_panel = t * (own * sign)

    def part(a, i):
        return a[:, i * W : (i + 1) * W]

    diag_terms = [dot(part(w_own, i), part(t, i), 0, 0) for i in range(4)]
    parent_terms = [dot(part(w_own, c), part(t, c + 2), 0, 0) for c in (0, 1)]
    terms = jnp.concatenate(
        [
            jnp.concatenate(diag_terms, axis=0).reshape(32, 32, W),
            jnp.concatenate(parent_terms, axis=0).reshape(32, 16, W),
        ],
        axis=1,
    ).reshape(32 * 48, W)
    base_parent = [dot(diag_inv[c * W : (c + 1) * W], v[c], 1, 0, HIGHEST) for c in (0, 1)]
    base_low = [dot(v[c], base_parent[c], 0, 0, HIGHEST) for c in (0, 1)]
    zero = jnp.zeros((2 * W, W), jnp.float32)
    base_diag = diag_inv + jnp.concatenate([zero] + base_low, axis=0)
    base_parent = jnp.concatenate(base_parent, axis=0)
    summed = sum_blocks(terms)
    cov_diag = lax.dynamic_slice_in_dim(base_diag, blk * 32, 32, 0) + summed[:32]
    cov_parent = -(lax.dynamic_slice_in_dim(base_parent, blk * 16, 16, 0) + summed[32:])
    return (cov_panel, cov_diag, cov_parent)


def solution(mesh):
    return jax.shard_map(
        per_device,
        mesh=mesh,
        in_specs=(P("grp", "blk"), P(("grp", "blk"), None), P(), P(), P(), P()),
        out_specs=(P(("blk", "grp"), None), P("blk", None), P("blk", None)),
        check_vma=False,
    )
```

time: 599 us -> 523 us (0.87)
  the two profiles are of different devices: /device:TPU:1 before, /device:TPU:2 now
where the time goes in v1:
time: 523 us
  waiting for transfers between devices  399 us (76%)
  blocking collectives  77.1 us (15%)
  matrix products  16.5 us (3%)
  between operations  13.9 us (3%)
  other arithmetic  7.11 us (1%)
  local copies, waits for them, and re-layouts  5.96 us (1%)
    unnamed x4, waiting for transfers between devices  210 us
    reduce_scatter x1, waiting for transfers between devices, sum_blocks(): lax.psum_scatter(terms, 'blk', scatter_dimension=0, tiled=True)  115 us
    psum x1, blocking collectives, sum_blocks(): lax.psum(lax.psum_scatter(terms, 'blk', scatter_dimension=0, tiled=True),...  77.1 us
    all_gather x1, waiting for transfers between devices, gather_rows(): return lax.all_gather(rows, 'blk', axis=0, tiled=True)  73.8 us
    dot_general x13, matrix products, dot(): lax.dot_general(a, b, (((ca,), (cb,)), ((), ())), precision=precision, pr...  16.5 us
  transfers between devices with their start and end apart: 4, of which 3 were waited for; matrix products, arithmetic and copies ran while one was open for 1% of the time, Pallas kernels for 0%

profile of v1, /device:TPU:2, one launch (start us, length us, event | category | flops | bytes accessed | tf_op | source)
XLA Modules:
  0.0 522.6 jit_solution(6177603634470408080)
XLA Ops:
  7.3 1.0 compare_reduce_fusion.1
  8.2 0.8 compare_reduce_fusion
  9.0 0.1 add_convert_fusion
  9.2 0.9 broadcast_multiply_fusion.1
  10.1 1.2 convolution_subtract_fusion
  11.3 1.2 convolution_subtract_fusion.1
  12.5 0.7 pad_maximum_fusion.3
  13.2 73.8 %all-gather.2.cloned.1.call-done = f32[1024,1024]{1,0:T(8,128)} async-done(((f32[32,1024]{1,0:T(8,128)}), f32[1024,1024]{1,0:T(8,128)}) %all-gather.2.cloned.1.call-update) | async-done | bytes 4194320 | tf_op jit(solution)/shard_map/all_gather | solution.py:25
  87.0 7.0 %convolution_bitcast_fusion = f32[512,1024]{0,1:T(8,128)} fusion(f32[1024,1024]{1,0:T(8,128)} %all-gather.2.cloned.1.call-done, f32[1024,512]{1,0:T(8,128)S(1)} %copy-done), kind=kOutput, calls=%fused_computation | convolution fusion | flops 3221225472 | bytes 8388608 | tf_op jit(solution)/shard_map/dot_general | solution.py:12
  94.0 2.9 copy.11
  97.0 0.8 copy-done.3
  97.8 2.9 collective-permute-start
  100.7 210.4 %reduce-scatter.7.cloned.1.call-done = f32[32,1024]{1,0:T(8,128)} async-done(((f32[512,1024]{1,0:T(8,128)}), f32[32,1024]{1,0:T(8,128)}) %reduce-scatter.7.cloned.1.call-update) | async-done | bytes 131088
  311.1 1.1 copy.12
  312.2 0.3 fusion.14
  312.5 0.3 fusion.18
  312.9 0.3 fusion.10
  313.2 0.3 fusion.12
  313.5 0.3 fusion.16
  313.9 0.3 fusion.20
  314.3 1.3 pad_maximum_fusion
  315.6 0.1 pad_dynamic-slice_fusion.4
  315.7 1.3 fusion
  317.1 1.3 fusion.2
  318.4 1.3 convolution_bitcast_fusion.1
  319.7 1.3 convolution_bitcast_fusion.2
  321.0 0.2 broadcast_multiply_fusion
  321.2 0.8 copy.10
  322.1 114.9 %reduce-scatter.5.cloned.1.call-done = f32[48,256]{1,0:T(8,128)} async-done(((f32[1536,256]{1,0:T(8,128)}), f32[48,256]{1,0:T(8,128)}) %reduce-scatter.5.cloned.1.call-update) | async-done | bytes 49168 | tf_op jit(solution)/shard_map/reduce_scatter | solution.py:33
  437.0 77.1 %psum.7 = f32[48,256]{1,0:T(8,128)S(1)} all-reduce(f32[48,256]{1,0:T(8,128)} %reduce-scatter.5.cloned.1.call-done), channel_id=1, replica_groups=mesh['grp'=16,'blk'=32] {'grp'}, use_global_device_ids=true, to_apply=%region_6.7 | all-reduce | flops 12288 | bytes 98304 | tf_op jit(solution)/shard_map/psum | solution.py:33
  514.0 0.6 fusion.32
  514.6 1.5 slice_add_fusion
  (23 shorter events, 0.5 us)
Async XLA Ops:
  7.2 79.8 %copy-start = (f32[1024,512]{1,0:T(8,128)S(1)}, f32[1024,512]{1,0:T(8,128)}, u32[]{:S(2)}) copy-start(f32[1024,512]{1,0:T(8,128)} %param.6) | copy-start | bytes 6291460
  7.2 79.8 %all-gather.2.cloned.1.call-start = ((), (), s32[]{:S(2)}) async-start(), calls=%async_computation.2 | async-start | bytes 4325376 | tf_op jit(solution)/shard_map/all_gather | solution.py:25
  13.2 297.9 %reduce-scatter.7.cloned.1.call-start = ((), (), s32[]{:S(2)}) async-start(), calls=%async_computation.4 | async-start | bytes 2228224
  96.9 0.9 copy-start.3
  96.9 340.0 %reduce-scatter.5.cloned.1.call-start = ((), (), s32[]{:S(2)}) async-start(), calls=%async_computation.3 | async-start | bytes 1622016 | tf_op jit(solution)/shard_map/reduce_scatter | solution.py:33
  97.8 214.3 %collective-permute-start = (f32[32,1024]{1,0:T(8,128)S(1)}, f32[32,1024]{1,0:T(8,128)S(1)}, u32[]{:S(2)}, u32[]{:S(2)}) collective-permute-start(f32[32,1024]{1,0:T(8,128)S(1)} %copy-done.3), channel_id=1, source_target_pairs={{0,0},{1,32},{2,64},{3,96},{4,128},{5,160},{6,192},{7,224},{8,256}... | collective-permute-start | bytes 393224 | tf_op jit(solution)/shard_map/ppermute | solution.py:44
  314.3 1.5 copy-start.1
  318.4 1.3 copy-start.2
Sparse Core Ops, SparseCore 0:
  13.3 73.6 all-gather.1
  97.1 213.9 reduce-scatter.6
  315.7 121.2 reduce-scatter.4

commit v2 on v1

--- a/solution.py
+++ b/solution.py
@@ -1,6 +1,8 @@
 import jax
 import jax.numpy as jnp
 from jax import lax
+from jax.experimental import pallas as pl
+from jax.experimental.pallas import tpu as pltpu
 from jax.sharding import PartitionSpec as P
 
 W = 256
@@ -21,16 +23,212 @@
     return jnp.repeat(flags, W)[None, :]
 
 
+VMEM = pl.BlockSpec(memory_space=pltpu.VMEM)
+DMA = pltpu.SemaphoreType.DMA
+
+
+def greet(axes_and_peers):
+    barrier = pltpu.get_barrier_semaphore()
+    for axis, peer in axes_and_peers:
+        pl.semaphore_signal(
+            barrier, inc=1, device_id={axis: peer}, device_id_type=pl.DeviceIdType.MESH
+        )
+    pl.semaphore_wait(barrier, len(axes_and_peers))
+
+
+def send(src, dst, send_sem, recv_sem, axis, peer):
+    copy = pltpu.make_async_remote_copy(
+        src_ref=src,
+        dst_ref=dst,
+        send_sem=send_sem,
+        recv_sem=recv_sem,
+        device_id={axis: peer},
+        device_id_type=pl.DeviceIdType.MESH,
+    )
+    copy.start()
+    return copy
+
+
+def call(kernel, out_shape, scratch, collective_id, operand, sent):
+    return pl.pallas_call(
+        kernel,
+        out_shape=jax.ShapeDtypeStruct(out_shape, jnp.float32),
+        in_specs=[VMEM],
+        out_specs=VMEM,
+        scratch_shapes=scratch,
+        cost_estimate=pl.CostEstimate(flops=1000000, bytes_accessed=sent, transcendentals=0),
+        compiler_params=pltpu.CompilerParams(
+            collective_id=collective_id, has_side_effects=True, vmem_limit_bytes=40 * 2**20
+        ),
+    )(operand)
+
+
+def gather_kernel(w_ref, o_ref, z_send, z_recv, x_send, x_recv, c_send, c_recv):
+    b = lax.axis_index("blk")
+    core, z, xl = b % 2, (b // 2) % 8, b // 16
+    across, sibling = (1 - xl) * 16 + z * 2 + core, xl * 16 + z * 2 + 1 - core
+    ring = [xl * 16 + ((z + 1) % 8) * 2 + core, xl * 16 + ((z + 7) % 8) * 2 + core]
+    greet([("blk", p) for p in ring + [across, sibling]])
+    copies = []
+    x_copy = send(w_ref, o_ref.at[xl, z, core], x_send, x_recv, "blk", across)
+
+    def share(src, dst, e, i):
+        copies.append(send(src, dst, c_send.at[e, i], c_recv.at[e, i], "blk", sibling))
+
+    hops = [[4, 3], [3, 4]]
+    travelling = {}
+    for s in range(5):
+        for e in range(2):
+            x = xl if e == 0 else 1 - xl
+            if s == 0:
+                if e == 1:
+                    x_copy.wait()
+                here = o_ref.at[x, z, core]
+                src = w_ref if e == 0 else here
+                for d in range(2):
+                    travelling[e, d] = send(
+                        src, here, z_send.at[e, d, 0], z_recv.at[e, d, 0], "blk", ring[d]
+                    )
+                share(src, here, e, 0)
+                continue
+            for d in range(2):
+                if s > hops[e][d]:
+                    continue
+                origin = (z + (8 - s)) % 8 if d == 0 else (z + s) % 8
+                here = o_ref.at[x, origin, core]
+                travelling[e, d].wait_recv()
+                copies_done = travelling[e, d]
+                copies.append((copies_done,))
+                if s < hops[e][d]:
+                    travelling[e, d] = send(
+                        here, here, z_send.at[e, d, s], z_recv.at[e, d, s], "blk", ring[d]
+                    )
+                share(here, here, e, 4 * d + s)
+    o_ref[xl, z, core] = w_ref[...]
+    for copy in copies:
+        if isinstance(copy, tuple):
+            copy[0].wait_send()
+        else:
+            copy.wait()
+
+
 def gather_rows(rows):
-    return lax.all_gather(rows, "blk", axis=0, tiled=True)
+    scratch = [DMA((2, 2, 4)), DMA((2, 2, 4)), DMA, DMA, DMA((2, 9)), DMA((2, 9))]
+    out = call(gather_kernel, (2, 8, 2, 32, 4 * W), scratch, 1, rows, 2**22)
+    return out.reshape(1024, 4 * W)
+
+
+def scatter_kernel(p_ref, o_ref, held, final, y_send, y_recv, x_send, x_recv):
+    g = lax.axis_index("grp")
+    y, h = g // 2, g % 2
+    ring = [((y + 1) % 8) * 2 + h, ((y + 7) % 8) * 2 + h]
+    across = y * 2 + 1 - h
+    greet([("grp", p) for p in ring + [across]])
+    copies = {}
+    for s in range(8):
+        for q in range(4):
+            columns = pl.ds(q * W, W)
+            chunk = (y + (7 - s)) % 8 if q % 2 == 0 else (y + 1 + s) % 8
+            rows = pl.ds(pl.multiple_of(chunk * 64, 64), 64)
+            if s == 0:
+                src = p_ref.at[rows, columns]
+            else:
+                copies[s - 1, q].wait_recv()
+                held[s - 1, q] = held[s - 1, q] + p_ref[rows, columns]
+                src = held.at[s - 1, q]
+            if s < 7:
+                copies[s, q] = send(
+                    src, held.at[s, q], y_send.at[s, q], y_recv.at[s, q], "grp", ring[q % 2]
+                )
+            else:
+                theirs = pl.ds(pl.multiple_of((1 - h) * 32, 32), 32)
+                copies[s, q] = send(
+                    held.at[6, q, theirs], final.at[q], x_send.at[q], x_recv.at[q], "grp", across
+                )
+    mine = pl.ds(pl.multiple_of(h * 32, 32), 32)
+    for q in range(4):
+        copies[7, q].wait_recv()
+        o_ref[:, q * W : (q + 1) * W] = held[6, q, mine] + final[q]
+    for copy in copies.values():
+        copy.wait_send()
 
 
 def scatter_products(partial):
-    return lax.psum_scatter(partial, "grp", scatter_dimension=0, tiled=True)
+    scratch = [
+        pltpu.VMEM((7, 4, 64, W), jnp.float32),
+        pltpu.VMEM((4, 32, W), jnp.float32),
+        DMA((7, 4)),
+        DMA((7, 4)),
+        DMA((4,)),
+        DMA((4,)),
+    ]
+    return call(scatter_kernel, (32, 4 * W), scratch, 2, partial, 2**22)
+
+
+def sum_kernel(t_ref, o_ref, pair, z_held, total, x_held, part, h_held, y_held, s_sem, r_sem):
+    g, b = lax.axis_index("grp"), lax.axis_index("blk")
+    y, h = g // 2, g % 2
+    core, z, xl = b % 2, (b // 2) % 8, b // 16
+    far_first = (4, 3, 5, 2, 6, 1, 7)
+    sibling, across = xl * 16 + z * 2 + 1 - core, (1 - xl) * 16 + z * 2 + core
+    z_peers = {d: xl * 16 + ((z + d) % 8) * 2 + core for d in far_first}
+    y_peers = {d: ((y + d) % 8) * 2 + h for d in far_first}
+    other = y * 2 + 1 - h
+    greet(
+        [("blk", sibling), ("blk", across), ("grp", other)]
+        + [("blk", z_peers[d]) for d in far_first]
+        + [("grp", y_peers[d]) for d in far_first]
+    )
+    copies = []
+
+    def pass_on(src, dst, i, axis, peer):
+        copies.append(send(src, dst, s_sem.at[i], r_sem.at[i], axis, peer))
+        return copies[-1]
+
+    first = {}
+    for d in far_first + (8,):
+        k = (z + d) % 8
+        first[d] = pass_on(t_ref.at[k, 1 - core], pair.at[k], 8 + d, "blk", sibling)
+    second = {}
+    for d in far_first:
+        k = (z + d) % 8
+        first[d].wait_recv()
+        pair[k] = pair[k] + t_ref[k, core]
+        second[d] = pass_on(pair.at[k], z_held.at[d - 1], d, "blk", z_peers[d])
+    first[8].wait_recv()
+    total[...] = pair[z] + t_ref[z, core]
+    for d in reversed(far_first):
+        second[d].wait_recv()
+        total[...] = total[...] + z_held[d - 1]
+    pass_on(total.at[1 - xl], x_held, 17, "blk", across).wait_recv()
+    part[...] = total[xl] + x_held[...]
+    pass_on(part, h_held, 18, "grp", other).wait_recv()
+    y_held[y] = part[...] + h_held[...]
+    third = [pass_on(y_held.at[y], y_held.at[y], 18 + d, "grp", y_peers[d]) for d in far_first]
+    for copy in third:
+        copy.wait_recv()
+    result = y_held[0]
+    for k in range(1, 8):
+        result = result + y_held[k]
+    o_ref[...] = result
+    for copy in copies:
+        copy.wait_send()
 
 
 def sum_blocks(terms):
-    return lax.psum(lax.psum_scatter(terms, "blk", scatter_dimension=0, tiled=True), "grp")
+    terms = terms.reshape(2, 8, 2, 48, W).transpose(1, 2, 0, 3, 4)
+    scratch = [
+        pltpu.VMEM((8, 2, 48, W), jnp.float32),
+        pltpu.VMEM((7, 2, 48, W), jnp.float32),
+        pltpu.VMEM((2, 48, W), jnp.float32),
+        pltpu.VMEM((48, W), jnp.float32),
+        pltpu.VMEM((48, W), jnp.float32),
+        pltpu.VMEM((48, W), jnp.float32),
+        pltpu.VMEM((8, 48, W), jnp.float32),
+        DMA((26,)),
+        DMA((26,)),
+    ]
+    return call(sum_kernel, (48, W), scratch, 3, terms, 2**22)
 
 
 def per_device(sigma_anc, panels, diag_inv, scaled_parent_panel, struct_upper, struct_lower):

time: 523 us -> 145 us (0.28)
  the two profiles are of different devices: /device:TPU:2 before, /device:TPU:1 now
where the time goes in v2:
time: 145 us; the launch traced here: 144 us
  Pallas kernels  122 us (84%)
  matrix products  9.6 us (7%)
  starting transfers between devices  6.16 us (4%)
  other arithmetic  5.84 us (4%)
    pallas_call x3, Pallas kernels, call(): pl.pallas_call(kernel, out_shape=jax.ShapeDtypeStruct(out_shape, jnp.floa...  122 us
    dot_general x13, matrix products, dot(): lax.dot_general(a, b, (((ca,), (cb,)), ((), ())), precision=precision, pr...  9.6 us
    ppermute x1, starting transfers between devices, per_device(): w_own = lax.ppermute(w, ('grp', 'blk'), moves)  6.16 us
  transfers between devices with their start and end apart: 1, of which 0 were waited for; matrix products, arithmetic and copies ran while one was open for 4% of the time, Pallas kernels for 51%

profile of v2, /device:TPU:1, one launch (start us, length us, event | category | flops | bytes accessed | tf_op | source)
XLA Modules:
  0.0 144.3 jit_solution(8282170035636935141)
XLA Ops:
  0.6 0.0 copy-start
  0.7 1.0 compare_reduce_fusion.1
  1.6 0.8 compare_reduce_fusion
  2.5 0.1 add_convert_fusion
  2.6 0.1 broadcast_bitcast_fusion.1
  2.6 0.9 broadcast_multiply_fusion.1
  3.6 1.2 convolution_subtract_fusion
  4.7 1.2 convolution_subtract_fusion.1
  5.9 0.0 copy-start.1
  5.9 0.0 copy-start.2
  5.9 6.2 %collective-permute-start = (f32[32,1024]{1,0:T(8,128)S(1)}, f32[32,1024]{1,0:T(8,128)S(1)}, u32[]{:S(2)}, u32[]{:S(2)}) collective-permute-start(f32[32,1024]{1,0:T(8,128)S(1)} %pad_maximum_fusion.3.w_ref), channel_id=1, source_target_pairs={{0,0},{1,32},{2,64},{3,96},{4,128},{5,160},{6,192},{7,224},{8,256}... | collective-permute-start | bytes 393224 | tf_op jit(solution)/shard_map/ppermute | solution.py:242
  12.1 39.8 %shard_map.85 = f32[2,8,2,32,1024]{4,3,2,1,0:T(8,128)S(1)} custom-call(f32[32,1024]{1,0:T(8,128)S(1)} %pad_maximum_fusion.3.w_ref), custom_call_target="tpu_custom_call" | custom-call | flops 1000000 | bytes 4194304 | tf_op jit(solution)/shard_map/pallas_call | solution.py:53
  51.9 0.4 fusion
  52.3 0.4 fusion.2
  52.7 3.5 %convolution_bitcast_fusion.p_ref = f32[512,1024]{1,0:T(8,128)S(1)} fusion(f32[1024,1024]{1,0:T(8,128)S(1)} %bitcast.21, f32[1024,512]{1,0:T(8,128)S(1)} %copy-done), kind=kOutput, calls=%fused_computation | convolution fusion | flops 3221225472 | bytes 8388608 | tf_op jit(solution)/shard_map/dot_general | solution.py:14
  56.2 33.3 %shard_map.86 = f32[32,1024]{1,0:T(8,128)S(1)} custom-call(f32[512,1024]{1,0:T(8,128)S(1)} %convolution_bitcast_fusion.p_ref), custom_call_target="tpu_custom_call" | custom-call | flops 1000000 | bytes 4194304 | tf_op jit(solution)/shard_map/pallas_call | solution.py:53
  89.5 0.6 convolution_bitcast_fusion.1
  90.1 0.6 convolution_bitcast_fusion.2
  90.7 0.1 broadcast_bitcast_fusion
  90.8 0.7 broadcast_multiply_fusion
  91.4 0.1 pad_dynamic-slice_fusion.4
  91.5 0.3 fusion.22
  91.8 0.3 fusion.25
  92.2 0.3 fusion.11
  92.5 0.3 fusion.13
  92.8 0.3 fusion.18
  93.2 0.3 fusion.20
  93.5 0.1 pad_maximum_fusion.1
  93.6 0.2 copy_bitcast_fusion.t_ref
  93.7 48.5 %shard_map.87 = f32[48,256]{1,0:T(8,128)S(1)} custom-call(f32[8,2,2,48,256]{4,3,2,1,0:T(8,128)S(1)} %copy_bitcast_fusion.t_ref), custom_call_target="tpu_custom_call" | custom-call | flops 1000000 | bytes 4194304 | tf_op jit(solution)/shard_map/pallas_call | solution.py:53
  142.3 0.6 add_negate_fusion
  142.9 1.4 %fusion.15 = f32[32,256]{1,0:T(8,128)} fusion(f32[1024,256]{1,0:T(8,128)} %param.8, s32[]{:T(128)S(6)} %select_n.25, f32[256,256]{1,0:T(8,128)S(1)} %convolution_bitcast_fusion.1, f32[48,256]{1,0:T(8,128)S(1)} %shard_map.87, f32[256,256]{1,0:T(8,128)S(1)} %convolution_bitcast_fusion.2, f32[32]{0:T(128)S(1)} %pad_dynamic-slice_fusion.4), kind=kLoop, calls=%fused_computation.32 | loop fusion | flops 32768 | bytes 622724 | tf_op jit(solution)/shard_map/add | solution.py:267
  (11 shorter events, 0.1 us)
Async XLA Ops:
  0.6 52.1 %copy-start = (f32[1024,512]{1,0:T(8,128)S(1)}, f32[1024,512]{1,0:T(8,128)}, u32[]{:S(2)}) copy-start(f32[1024,512]{1,0:T(8,128)} %param.6) | copy-start | bytes 6291460
  5.9 46.0 %copy-start.1 = (f32[512,256]{1,0:T(8,128)S(1)}, f32[512,256]{1,0:T(8,128)}, u32[]{:S(2)}) copy-start(f32[512,256]{1,0:T(8,128)} %param.9) | copy-start | bytes 1572868
  5.9 46.0 %copy-start.2 = (f32[1024,256]{1,0:T(8,128)S(1)}, f32[1024,256]{1,0:T(8,128)}, u32[]{:S(2)}) copy-start(f32[1024,256]{1,0:T(8,128)} %param.8) | copy-start | bytes 3145732
  5.9 85.6 %collective-permute-start = (f32[32,1024]{1,0:T(8,128)S(1)}, f32[32,1024]{1,0:T(8,128)S(1)}, u32[]{:S(2)}, u32[]{:S(2)}) collective-permute-start(f32[32,1024]{1,0:T(8,128)S(1)} %pad_maximum_fusion.3.w_ref), channel_id=1, source_target_pairs={{0,0},{1,32},{2,64},{3,96},{4,128},{5,160},{6,192},{7,224},{8,256}... | collective-permute-start | bytes 393224 | tf_op jit(solution)/shard_map/ppermute | solution.py:242

commit v3 on v2

--- a/solution.py
+++ b/solution.py
@@ -49,31 +49,30 @@
     return copy
 
 
-def call(kernel, out_shape, scratch, collective_id, operand, sent):
+def call(kernel, out_shape, scratch, collective_id, operands, sent):
     return pl.pallas_call(
         kernel,
         out_shape=jax.ShapeDtypeStruct(out_shape, jnp.float32),
-        in_specs=[VMEM],
+        in_specs=[VMEM] * len(operands),
         out_specs=VMEM,
         scratch_shapes=scratch,
         cost_estimate=pl.CostEstimate(flops=1000000, bytes_accessed=sent, transcendentals=0),
         compiler_params=pltpu.CompilerParams(
             collective_id=collective_id, has_side_effects=True, vmem_limit_bytes=40 * 2**20
         ),
-    )(operand)
-
-
-def gather_kernel(w_ref, o_ref, z_send, z_recv, x_send, x_recv, c_send, c_recv):
-    b = lax.axis_index("blk")
-    core, z, xl = b % 2, (b // 2) % 8, b // 16
+    )(*operands)
+
+
+def gather_steps(w_ref, o_ref, columns, ids, z_send, z_recv, x_send, x_recv, c_send, c_recv):
+    core, z, xl = ids
     across, sibling = (1 - xl) * 16 + z * 2 + core, xl * 16 + z * 2 + 1 - core
     ring = [xl * 16 + ((z + 1) % 8) * 2 + core, xl * 16 + ((z + 7) % 8) * 2 + core]
-    greet([("blk", p) for p in ring + [across, sibling]])
-    copies = []
-    x_copy = send(w_ref, o_ref.at[xl, z, core], x_send, x_recv, "blk", across)
+    own = w_ref.at[:, columns]
+    arriving, leaving = [], []
+    x_copy = send(own, o_ref.at[xl, z, core], x_send, x_recv, "blk", across)
 
     def share(src, dst, e, i):
-        copies.append(send(src, dst, c_send.at[e, i], c_recv.at[e, i], "blk", sibling))
+        arriving.append(send(src, dst, c_send.at[e, i], c_recv.at[e, i], "blk", sibling))
 
     hops = [[4, 3], [3, 4]]
     travelling = {}
@@ -82,13 +81,15 @@
             x = xl if e == 0 else 1 - xl
             if s == 0:
                 if e == 1:
+                    yield
                     x_copy.wait()
                 here = o_ref.at[x, z, core]
-                src = w_ref if e == 0 else here
+                src = own if e == 0 else here
                 for d in range(2):
                     travelling[e, d] = send(
                         src, here, z_send.at[e, d, 0], z_recv.at[e, d, 0], "blk", ring[d]
                     )
+                    leaving.append(travelling[e, d])
                 share(src, here, e, 0)
                 continue
             for d in range(2):
@@ -97,44 +98,35 @@
                 origin = (z + (8 - s)) % 8 if d == 0 else (z + s) % 8
                 here = o_ref.at[x, origin, core]
                 travelling[e, d].wait_recv()
-                copies_done = travelling[e, d]
-                copies.append((copies_done,))
                 if s < hops[e][d]:
                     travelling[e, d] = send(
                         here, here, z_send.at[e, d, s], z_recv.at[e, d, s], "blk", ring[d]
                     )
+                    leaving.append(travelling[e, d])
                 share(here, here, e, 4 * d + s)
-    o_ref[xl, z, core] = w_ref[...]
-    for copy in copies:
-        if isinstance(copy, tuple):
-            copy[0].wait_send()
-        else:
-            copy.wait()
-
-
-def gather_rows(rows):
-    scratch = [DMA((2, 2, 4)), DMA((2, 2, 4)), DMA, DMA, DMA((2, 9)), DMA((2, 9))]
-    out = call(gather_kernel, (2, 8, 2, 32, 4 * W), scratch, 1, rows, 2**22)
-    return out.reshape(1024, 4 * W)
-
-
-def scatter_kernel(p_ref, o_ref, held, final, y_send, y_recv, x_send, x_recv):
-    g = lax.axis_index("grp")
-    y, h = g // 2, g % 2
+        yield
+    o_ref[xl, z, core] = w_ref[:, columns]
+    for copy in leaving:
+        copy.wait_send()
+    for copy in arriving:
+        copy.wait()
+
+
+def scatter_steps(p_ref, o_ref, first, held, final, ids, y_send, y_recv, x_send, x_recv):
+    y, h = ids
     ring = [((y + 1) % 8) * 2 + h, ((y + 7) % 8) * 2 + h]
     across = y * 2 + 1 - h
-    greet([("grp", p) for p in ring + [across]])
+    width = W // 2
     copies = {}
     for s in range(8):
         for q in range(4):
-            columns = pl.ds(q * W, W)
+            columns = pl.ds(q * width, width)
             chunk = (y + (7 - s)) % 8 if q % 2 == 0 else (y + 1 + s) % 8
-            rows = pl.ds(pl.multiple_of(chunk * 64, 64), 64)
             if s == 0:
-                src = p_ref.at[rows, columns]
+                src = p_ref.at[chunk, :, columns]
             else:
                 copies[s - 1, q].wait_recv()
-                held[s - 1, q] = held[s - 1, q] + p_ref[rows, columns]
+                held[s - 1, q] = held[s - 1, q] + p_ref[chunk, :, columns]
                 src = held.at[s - 1, q]
             if s < 7:
                 copies[s, q] = send(
@@ -145,24 +137,117 @@
                 copies[s, q] = send(
                     held.at[6, q, theirs], final.at[q], x_send.at[q], x_recv.at[q], "grp", across
                 )
+        yield
     mine = pl.ds(pl.multiple_of(h * 32, 32), 32)
     for q in range(4):
         copies[7, q].wait_recv()
-        o_ref[:, q * W : (q + 1) * W] = held[6, q, mine] + final[q]
+        o_ref[:, first + q * width : first + (q + 1) * width] = held[6, q, mine] + final[q]
     for copy in copies.values():
         copy.wait_send()
 
 
-def scatter_products(partial):
+def split(value):
+    high = value.astype(jnp.bfloat16)
+    return high, (value - high.astype(jnp.float32)).astype(jnp.bfloat16)
+
+
+def product_kernel(
+    s_ref, w_ref, o_ref, rows, s_high, s_low, r_high, r_low, partial, held, final, *sems
+):
+    g, b = lax.axis_index("grp"), lax.axis_index("blk")
+    y, h = g // 2, g % 2
+    core, z, xl = b % 2, (b // 2) % 8, b // 16
+    greet(
+        [
+            ("blk", xl * 16 + ((z + 1) % 8) * 2 + core),
+            ("blk", xl * 16 + ((z + 7) % 8) * 2 + core),
+            ("blk", (1 - xl) * 16 + z * 2 + core),
+            ("blk", xl * 16 + z * 2 + 1 - core),
+            ("grp", ((y + 1) % 8) * 2 + h),
+            ("grp", ((y + 7) % 8) * 2 + h),
+            ("grp", y * 2 + 1 - h),
+        ]
+    )
+    g_sems, y_sems = sems[:6], sems[6:]
+
+    def at(refs, half):
+        return [ref.at[half] for ref in refs]
+
+    gathers = [
+        gather_steps(
+            w_ref, rows.at[i], pl.ds(i * 2 * W, 2 * W), (core, z, xl), *at(g_sems, i)
+        )
+        for i in range(2)
+    ]
+    scatters = [
+        scatter_steps(
+            partial.at[i], o_ref, i * 2 * W, held.at[i], final.at[i], (y, h), *at(y_sems, i)
+        )
+        for i in range(2)
+    ]
+
+    def product(half):
+        high, low = split(rows[half].reshape(1024, 2 * W))
+        r_high[...] = high
+        r_low[...] = low
+
+        @pl.loop(0, 4)
+        def _(m):
+            some = pl.ds(pl.multiple_of(m * 128, 128), 128)
+
+            def mul(p, q):
+                return jnp.dot(p[some, :], q[...], preferred_element_type=jnp.float32)
+
+            total = mul(s_high, r_low) + mul(s_low, r_high) + mul(s_high, r_high)
+            partial[half, pl.ds(m * 2, 2)] = total.reshape(2, 64, 2 * W)
+
+    def step(steps):
+        next(steps, None)
+
+    step(gathers[0])
+    for i in range(8):
+        some = slice(i * 128, (i + 1) * 128)
+        s_high[:, some], s_low[:, some] = split(s_ref[some, :].T)
+    for _ in range(4):
+        step(gathers[0])
+    step(gathers[1])
+    step(gathers[0])
+    step(gathers[1])
+    step(gathers[0])
+    product(0)
+    step(scatters[0])
+    for _ in range(5):
+        step(gathers[1])
+        step(scatters[0])
+    product(1)
+    for _ in range(9):
+        step(scatters[1])
+        step(scatters[0])
+
+
+def products(sigma, rows):
+    f32, bf16 = jnp.float32, jnp.bfloat16
     scratch = [
-        pltpu.VMEM((7, 4, 64, W), jnp.float32),
-        pltpu.VMEM((4, 32, W), jnp.float32),
-        DMA((7, 4)),
-        DMA((7, 4)),
-        DMA((4,)),
-        DMA((4,)),
+        pltpu.VMEM((2, 2, 8, 2, 32, 2 * W), f32),
+        pltpu.VMEM((512, 1024), bf16),
+        pltpu.VMEM((512, 1024), bf16),
+        pltpu.VMEM((1024, 2 * W), bf16),
+        pltpu.VMEM((1024, 2 * W), bf16),
+        pltpu.VMEM((2, 8, 64, 2 * W), f32),
+        pltpu.VMEM((2, 7, 4, 64, W // 2), f32),
+        pltpu.VMEM((2, 4, 32, W // 2), f32),
+        DMA((2, 2, 2, 4)),
+        DMA((2, 2, 2, 4)),
+        DMA((2,)),
+        DMA((2,)),
+        DMA((2, 2, 9)),
+        DMA((2, 2, 9)),
+        DMA((2, 7, 4)),
+        DMA((2, 7, 4)),
+        DMA((2, 4)),
+        DMA((2, 4)),
     ]
-    return call(scatter_kernel, (32, 4 * W), scratch, 2, partial, 2**22)
+    return call(product_kernel, (32, 4 * W), scratch, 1, [sigma, rows], 2**23)
 
 
 def sum_kernel(t_ref, o_ref, pair, z_held, total, x_held, part, h_held, y_held, s_sem, r_sem):
@@ -228,7 +313,7 @@
         DMA((26,)),
         DMA((26,)),
     ]
-    return call(sum_kernel, (48, W), scratch, 3, terms, 2**22)
+    return call(sum_kernel, (48, W), scratch, 3, [terms], 2**22)
 
 
 def per_device(sigma_anc, panels, diag_inv, scaled_parent_panel, struct_upper, struct_lower):
@@ -240,8 +325,7 @@
     w = jnp.concatenate([u[:, : 2 * W], x[0], x[1]], axis=1)
     moves = [(q, (q % 16) * 32 + q // 16) for q in range(512)]
     w_own = lax.ppermute(w, ("grp", "blk"), moves)
-    gathered = gather_rows(w)
-    t = scatter_products(dot(sigma_anc, gathered, 0, 0))
+    t = products(sigma_anc, w)
     own = listed(struct_upper, struct_lower, (blk * 16 + grp) // 8)
     sign = jnp.where(jnp.arange(4 * W) < 2 * W, -1.0, 1.0).astype(jnp.float32)[None, :]
     cov_panel = t * (own * sign)

time: 145 us -> 150 us (1.034)
  Pallas kernels: 122 us -> 129 us
  matrix products: 9.6 us -> 8.02 us
    pallas_call x3 -> x2, Pallas kernels: 122 us -> 129 us  [call(): pl.pallas_call(kernel, out_shape=jax.ShapeDtypeStruct(out_shape, jnp.floa...]
    dot_general x13 -> x12, matrix products: 9.6 us -> 8.02 us  [dot(): lax.dot_general(a, b, (((ca,), (cb,)), ((), ())), precision=precision, pr...]
  transfers between devices with their start and end apart: 1 -> 1, of which waited for: 0 -> 0; matrix products, arithmetic and copies ran while one was open for 4% -> 3% of each run, Pallas kernels for 51% -> 53%
where the time goes in v3:
time: 150 us
  Pallas kernels  129 us (86%)
  matrix products  8.02 us (5%)
  starting transfers between devices  6.03 us (4%)
  other arithmetic  5.84 us (4%)
    pallas_call x2, Pallas kernels, call(): pl.pallas_call(kernel, out_shape=jax.ShapeDtypeStruct(out_shape, jnp.floa...  129 us
    dot_general x12, matrix products, dot(): lax.dot_general(a, b, (((ca,), (cb,)), ((), ())), precision=precision, pr...  8.02 us
    ppermute x1, starting transfers between devices, per_device(): w_own = lax.ppermute(w, ('grp', 'blk'), moves)  6.03 us
  transfers between devices with their start and end apart: 1, of which 0 were waited for; matrix products, arithmetic and copies ran while one was open for 3% of the time, Pallas kernels for 53%

profile of v3, /device:TPU:1, one launch (start us, length us, event | category | flops | bytes accessed | tf_op | source)
XLA Modules:
  0.0 150.1 jit_solution(2422678715550594249)
XLA Ops:
  0.6 0.0 copy-start.1
  0.6 0.0 copy-start
  0.7 1.0 compare_reduce_fusion.1
  1.7 0.8 compare_reduce_fusion
  2.5 0.1 add_convert_fusion
  2.6 0.1 broadcast_bitcast_fusion.1
  2.6 0.9 broadcast_multiply_fusion.1
  3.6 1.2 convolution_subtract_fusion
  4.8 1.2 convolution_subtract_fusion.1
  5.9 6.0 %collective-permute-start = (f32[32,1024]{1,0:T(8,128)S(1)}, f32[32,1024]{1,0:T(8,128)S(1)}, u32[]{:S(2)}, u32[]{:S(2)}) collective-permute-start(f32[32,1024]{1,0:T(8,128)S(1)} %pad_maximum_fusion.3.w_ref), channel_id=1, source_target_pairs={{0,0},{1,32},{2,64},{3,96},{4,128},{5,160},{6,192},{7,224},{8,256}... | collective-permute-start | bytes 393224 | tf_op jit(solution)/shard_map/ppermute | solution.py:327
  12.0 0.0 copy-done.1
  12.0 1.3 fusion
  13.3 1.3 fusion.2
  14.7 0.0 copy-done
  14.7 79.4 %shard_map.85 = f32[32,1024]{1,0:T(8,128)S(1)} custom-call(f32[1024,512]{1,0:T(8,128)S(1)} %copy-done, f32[32,1024]{1,0:T(8,128)S(1)} %pad_maximum_fusion.3.w_ref), custom_call_target="tpu_custom_call" | custom-call | flops 1000000 | bytes 8388608 | tf_op jit(solution)/shard_map/pallas_call | solution.py:53
  94.1 0.6 convolution_bitcast_fusion
  94.7 0.6 convolution_bitcast_fusion.1
  95.3 0.1 broadcast_bitcast_fusion
  95.4 0.7 broadcast_multiply_fusion
  96.0 0.1 pad_dynamic-slice_fusion.4
  96.1 0.0 collective-permute-done
  96.1 0.3 fusion.22
  96.4 0.3 fusion.25
  96.8 0.3 fusion.11
  97.1 0.3 fusion.13
  97.4 0.3 fusion.18
  97.8 0.3 fusion.20
  98.1 0.1 pad_maximum_fusion.1
  98.2 0.2 copy_bitcast_fusion.t_ref
  98.3 49.7 %shard_map.86 = f32[48,256]{1,0:T(8,128)S(1)} custom-call(f32[8,2,2,48,256]{4,3,2,1,0:T(8,128)S(1)} %copy_bitcast_fusion.t_ref), custom_call_target="tpu_custom_call" | custom-call | flops 1000000 | bytes 4194304 | tf_op jit(solution)/shard_map/pallas_call | solution.py:53
  148.0 0.6 add_negate_fusion
  148.6 1.4 fusion.15
  (7 shorter events, 0.1 us)
Async XLA Ops:
  0.6 11.3 %copy-start.1 = (f32[512,256]{1,0:T(8,128)S(1)}, f32[512,256]{1,0:T(8,128)}, u32[]{:S(2)}) copy-start(f32[512,256]{1,0:T(8,128)} %param.9) | copy-start | bytes 1572868
  0.6 14.0 %copy-start = (f32[1024,512]{1,0:T(8,128)S(1)}, f32[1024,512]{1,0:T(8,128)}, u32[]{:S(2)}) copy-start(f32[1024,512]{1,0:T(8,128)} %s_ref.1) | copy-start | bytes 6291460
  5.9 90.2 %collective-permute-start = (f32[32,1024]{1,0:T(8,128)S(1)}, f32[32,1024]{1,0:T(8,128)S(1)}, u32[]{:S(2)}, u32[]{:S(2)}) collective-permute-start(f32[32,1024]{1,0:T(8,128)S(1)} %pad_maximum_fusion.3.w_ref), channel_id=1, source_target_pairs={{0,0},{1,32},{2,64},{3,96},{4,128},{5,160},{6,192},{7,224},{8,256}... | collective-permute-start | bytes 393224 | tf_op jit(solution)/shard_map/ppermute | solution.py:327

commit v4 on v2

--- a/solution.py
+++ b/solution.py
@@ -49,18 +49,18 @@
     return copy
 
 
-def call(kernel, out_shape, scratch, collective_id, operand, sent):
+def call(kernel, out_shapes, scratch, collective_id, operands, sent):
     return pl.pallas_call(
         kernel,
-        out_shape=jax.ShapeDtypeStruct(out_shape, jnp.float32),
-        in_specs=[VMEM],
-        out_specs=VMEM,
+        out_shape=[jax.ShapeDtypeStruct(shape, jnp.float32) for shape in out_shapes],
+        in_specs=[VMEM] * len(operands),
+        out_specs=[VMEM] * len(out_shapes),
         scratch_shapes=scratch,
         cost_estimate=pl.CostEstimate(flops=1000000, bytes_accessed=sent, transcendentals=0),
         compiler_params=pltpu.CompilerParams(
             collective_id=collective_id, has_side_effects=True, vmem_limit_bytes=40 * 2**20
         ),
-    )(operand)
+    )(*operands)
 
 
 def gather_kernel(w_ref, o_ref, z_send, z_recv, x_send, x_recv, c_send, c_recv):
@@ -114,17 +114,35 @@
 
 def gather_rows(rows):
     scratch = [DMA((2, 2, 4)), DMA((2, 2, 4)), DMA, DMA, DMA((2, 9)), DMA((2, 9))]
-    out = call(gather_kernel, (2, 8, 2, 32, 4 * W), scratch, 1, rows, 2**22)
+    (out,) = call(gather_kernel, [(2, 8, 2, 32, 4 * W)], scratch, 1, [rows], 2**22)
     return out.reshape(1024, 4 * W)
 
 
-def scatter_kernel(p_ref, o_ref, held, final, y_send, y_recv, x_send, x_recv):
-    g = lax.axis_index("grp")
+def split(value):
+    high = value.astype(jnp.bfloat16)
+    return high, (value - high.astype(jnp.float32)).astype(jnp.bfloat16)
+
+
+def tail_kernel(
+    p_ref, u_ref, base_ref, o_ref, diag_ref, parent_ref,
+    held, final, u_high, u_low, t_ref, pair, z_held, total, x_held, part, h_held, y_held,
+    y_send, y_recv, x_send, x_recv, s_sem, r_sem,
+):
+    g, b = lax.axis_index("grp"), lax.axis_index("blk")
     y, h = g // 2, g % 2
-    ring = [((y + 1) % 8) * 2 + h, ((y + 7) % 8) * 2 + h]
-    across = y * 2 + 1 - h
-    greet([("grp", p) for p in ring + [across]])
-    copies = {}
+    core, z, xl = b % 2, (b // 2) % 8, b // 16
+    far_first = (4, 3, 5, 2, 6, 1, 7)
+    sibling, across = xl * 16 + z * 2 + 1 - core, (1 - xl) * 16 + z * 2 + core
+    z_peers = {d: xl * 16 + ((z + d) % 8) * 2 + core for d in far_first}
+    y_peers = {d: ((y + d) % 8) * 2 + h for d in far_first}
+    ring = [y_peers[1], y_peers[7]]
+    other = y * 2 + 1 - h
+    greet(
+        [("blk", sibling), ("blk", across), ("grp", other)]
+        + [("blk", z_peers[d]) for d in far_first]
+        + [("grp", y_peers[d]) for d in far_first]
+    )
+    ring_copies = {}
     for s in range(8):
         for q in range(4):
             columns = pl.ds(q * W, W)
@@ -133,52 +151,41 @@
             if s == 0:
                 src = p_ref.at[rows, columns]
             else:
-                copies[s - 1, q].wait_recv()
+                ring_copies[s - 1, q].wait_recv()
                 held[s - 1, q] = held[s - 1, q] + p_ref[rows, columns]
                 src = held.at[s - 1, q]
             if s < 7:
-                copies[s, q] = send(
+                ring_copies[s, q] = send(
                     src, held.at[s, q], y_send.at[s, q], y_recv.at[s, q], "grp", ring[q % 2]
                 )
             else:
                 theirs = pl.ds(pl.multiple_of((1 - h) * 32, 32), 32)
-                copies[s, q] = send(
-                    held.at[6, q, theirs], final.at[q], x_send.at[q], x_recv.at[q], "grp", across
+                ring_copies[s, q] = send(
+                    held.at[6, q, theirs], final.at[q], x_send.at[q], x_recv.at[q], "grp", other
                 )
+        if s == 0:
+            for q in range(4):
+                u_high[q], u_low[q] = split(u_ref[:, q * W : (q + 1) * W].T)
     mine = pl.ds(pl.multiple_of(h * 32, 32), 32)
     for q in range(4):
-        copies[7, q].wait_recv()
-        o_ref[:, q * W : (q + 1) * W] = held[6, q, mine] + final[q]
-    for copy in copies.values():
-        copy.wait_send()
-
-
-def scatter_products(partial):
-    scratch = [
-        pltpu.VMEM((7, 4, 64, W), jnp.float32),
-        pltpu.VMEM((4, 32, W), jnp.float32),
-        DMA((7, 4)),
-        DMA((7, 4)),
-        DMA((4,)),
-        DMA((4,)),
-    ]
-    return call(scatter_kernel, (32, 4 * W), scratch, 2, partial, 2**22)
-
-
-def sum_kernel(t_ref, o_ref, pair, z_held, total, x_held, part, h_held, y_held, s_sem, r_sem):
-    g, b = lax.axis_index("grp"), lax.axis_index("blk")
-    y, h = g // 2, g % 2
-    core, z, xl = b % 2, (b // 2) % 8, b // 16
-    far_first = (4, 3, 5, 2, 6, 1, 7)
-    sibling, across = xl * 16 + z * 2 + 1 - core, (1 - xl) * 16 + z * 2 + core
-    z_peers = {d: xl * 16 + ((z + d) % 8) * 2 + core for d in far_first}
-    y_peers = {d: ((y + d) % 8) * 2 + h for d in far_first}
-    other = y * 2 + 1 - h
-    greet(
-        [("blk", sibling), ("blk", across), ("grp", other)]
-        + [("blk", z_peers[d]) for d in far_first]
-        + [("grp", y_peers[d]) for d in far_first]
-    )
+        ring_copies[7, q].wait_recv()
+        piece = held[6, q, mine] + final[q]
+        o_ref[:, q * W : (q + 1) * W] = piece
+        high, low = split(piece)
+
+        def product(i):
+            def mul(p, r):
+                return jnp.dot(p[i], r, preferred_element_type=jnp.float32)
+
+            return mul(u_high, low) + mul(u_low, high) + mul(u_high, high)
+
+        diag = product(q)
+        for j in range(8):
+            t_ref[4 * (q % 2) + j // 2, j % 2, q // 2, :32] = diag[j * 32 : (j + 1) * 32]
+        if q >= 2:
+            mixed = product(q - 2)
+            for j in range(16):
+                t_ref[j // 2, j % 2, q - 2, 32:] = mixed[j * 16 : (j + 1) * 16]
     copies = []
 
     def pass_on(src, dst, i, axis, peer):
@@ -210,25 +217,37 @@
     result = y_held[0]
     for k in range(1, 8):
         result = result + y_held[k]
-    o_ref[...] = result
-    for copy in copies:
+    result = result + base_ref[...]
+    diag_ref[...] = result[:32]
+    parent_ref[...] = -result[32:]
+    for copy in copies + list(ring_copies.values()):
         copy.wait_send()
 
 
-def sum_blocks(terms):
-    terms = terms.reshape(2, 8, 2, 48, W).transpose(1, 2, 0, 3, 4)
+def scatter_and_sum(partial, w_own, base):
+    f32, bf16 = jnp.float32, jnp.bfloat16
     scratch = [
-        pltpu.VMEM((8, 2, 48, W), jnp.float32),
-        pltpu.VMEM((7, 2, 48, W), jnp.float32),
-        pltpu.VMEM((2, 48, W), jnp.float32),
-        pltpu.VMEM((48, W), jnp.float32),
-        pltpu.VMEM((48, W), jnp.float32),
-        pltpu.VMEM((48, W), jnp.float32),
-        pltpu.VMEM((8, 48, W), jnp.float32),
+        pltpu.VMEM((7, 4, 64, W), f32),
+        pltpu.VMEM((4, 32, W), f32),
+        pltpu.VMEM((4, W, 32), bf16),
+        pltpu.VMEM((4, W, 32), bf16),
+        pltpu.VMEM((8, 2, 2, 48, W), f32),
+        pltpu.VMEM((8, 2, 48, W), f32),
+        pltpu.VMEM((7, 2, 48, W), f32),
+        pltpu.VMEM((2, 48, W), f32),
+        pltpu.VMEM((48, W), f32),
+        pltpu.VMEM((48, W), f32),
+        pltpu.VMEM((48, W), f32),
+        pltpu.VMEM((8, 48, W), f32),
+        DMA((7, 4)),
+        DMA((7, 4)),
+        DMA((4,)),
+        DMA((4,)),
         DMA((26,)),
         DMA((26,)),
     ]
-    return call(sum_kernel, (48, W), scratch, 3, terms, 2**22)
+    shapes = [(32, 4 * W), (32, W), (16, W)]
+    return call(tail_kernel, shapes, scratch, 2, [partial, w_own, base], 2**23)
 
 
 def per_device(sigma_anc, panels, diag_inv, scaled_parent_panel, struct_upper, struct_lower):
@@ -241,31 +260,22 @@
     moves = [(q, (q % 16) * 32 + q // 16) for q in range(512)]
     w_own = lax.ppermute(w, ("grp", "blk"), moves)
     gathered = gather_rows(w)
-    t = scatter_products(dot(sigma_anc, gathered, 0, 0))
-    own = listed(struct_upper, struct_lower, (blk * 16 + grp) // 8)
-    sign = jnp.where(jnp.arange(4 * W) < 2 * W, -1.0, 1.0).astype(jnp.float32)[None, :]
-    cov_panel = t * (own * sign)
-
-    def part(a, i):
-        return a[:, i * W : (i + 1) * W]
-
-    diag_terms = [dot(part(w_own, i), part(t, i), 0, 0) for i in range(4)]
-    parent_terms = [dot(part(w_own, c), part(t, c + 2), 0, 0) for c in (0, 1)]
-    terms = jnp.concatenate(
-        [
-            jnp.concatenate(diag_terms, axis=0).reshape(32, 32, W),
-            jnp.concatenate(parent_terms, axis=0).reshape(32, 16, W),
-        ],
-        axis=1,
-    ).reshape(32 * 48, W)
     base_parent = [dot(diag_inv[c * W : (c + 1) * W], v[c], 1, 0, HIGHEST) for c in (0, 1)]
     base_low = [dot(v[c], base_parent[c], 0, 0, HIGHEST) for c in (0, 1)]
     zero = jnp.zeros((2 * W, W), jnp.float32)
     base_diag = diag_inv + jnp.concatenate([zero] + base_low, axis=0)
-    base_parent = jnp.concatenate(base_parent, axis=0)
-    summed = sum_blocks(terms)
-    cov_diag = lax.dynamic_slice_in_dim(base_diag, blk * 32, 32, 0) + summed[:32]
-    cov_parent = -(lax.dynamic_slice_in_dim(base_parent, blk * 16, 16, 0) + summed[32:])
+    base = jnp.concatenate(
+        [
+            lax.dynamic_slice_in_dim(base_diag, blk * 32, 32, 0),
+            lax.dynamic_slice_in_dim(jnp.concatenate(base_parent, axis=0), blk * 16, 16, 0),
+        ],
+        axis=0,
+    )
+    partial = dot(sigma_anc, gathered, 0, 0)
+    t, cov_diag, cov_parent = scatter_and_sum(partial, w_own, base)
+    own = listed(struct_upper, struct_lower, (blk * 16 + grp) // 8)
+    sign = jnp.where(jnp.arange(4 * W) < 2 * W, -1.0, 1.0).astype(jnp.float32)[None, :]
+    cov_panel = t * (own * sign)
     return (cov_panel, cov_diag, cov_parent)
 
 

time: 145 us -> 150 us (1.034)
  matrix products: 9.6 us -> 14.6 us
  local copies, waits for them, and re-layouts: 0.26 us -> 4.98 us
  Pallas kernels: 122 us -> 119 us
  other arithmetic: 5.84 us -> 4.34 us
    dot_general x13 -> x7, matrix products: 9.6 us -> 14.6 us  [dot(): lax.dot_general(a, b, (((ca,), (cb,)), ((), ())), precision=precision, pr...]
    unnamed x10 -> x18, local copies, waits for them, and re-layouts: 0.18 us -> 4.9 us
    pallas_call x3 -> x2, Pallas kernels: 122 us -> 119 us  [call(): pl.pallas_call(kernel, out_shape=[jax.ShapeDtypeStruct(shape, jnp.float32...]
  transfers between devices with their start and end apart: 1 -> 1, of which waited for: 0 -> 0; matrix products, arithmetic and copies ran while one was open for 4% -> 9% of each run, Pallas kernels for 51% -> 27%
where the time goes in v4:
time: 150 us
  Pallas kernels  119 us (79%)
  matrix products  14.6 us (10%)
  starting transfers between devices  6.16 us (4%)
  local copies, waits for them, and re-layouts  4.98 us (3%)
  other arithmetic  4.34 us (3%)
    pallas_call x2, Pallas kernels, call(): pl.pallas_call(kernel, out_shape=[jax.ShapeDtypeStruct(shape, jnp.float32...  119 us
    dot_general x7, matrix products, dot(): lax.dot_general(a, b, (((ca,), (cb,)), ((), ())), precision=precision, pr...  14.6 us
    ppermute x1, starting transfers between devices, per_device(): w_own = lax.ppermute(w, ('grp', 'blk'), moves)  6.16 us
    unnamed x18, local copies, waits for them, and re-layouts  4.9 us
  transfers between devices with their start and end apart: 1, of which 0 were waited for; matrix products, arithmetic and copies ran while one was open for 9% of the time, Pallas kernels for 27%

profile of v4, /device:TPU:1, one launch (start us, length us, event | category | flops | bytes accessed | tf_op | source)
XLA Modules:
  0.0 149.9 jit_solution(4340829685057882322)
XLA Ops:
  0.6 0.0 copy-start
  0.7 1.0 compare_reduce_fusion.1
  1.6 0.8 compare_reduce_fusion
  2.5 0.1 add_convert_fusion
  2.6 0.1 broadcast_bitcast_fusion.1
  2.6 0.9 broadcast_multiply_fusion.1
  3.6 1.2 convolution_subtract_fusion
  4.7 1.2 convolution_subtract_fusion.1
  5.9 0.0 copy-start.3
  5.9 6.2 %collective-permute-start = (f32[32,1024]{1,0:T(8,128)S(1)}, f32[32,1024]{1,0:T(8,128)S(1)}, u32[]{:S(2)}, u32[]{:S(2)}) collective-permute-start(f32[32,1024]{1,0:T(8,128)S(1)} %pad_maximum_fusion.w_ref), channel_id=1, source_target_pairs={{0,0},{1,32},{2,64},{3,96},{4,128},{5,160},{6,192},{7,224},{8,256}... | collective-permute-start | bytes 393224 | tf_op jit(solution)/shard_map/ppermute | solution.py:261
  12.1 39.8 %shard_map.85 = f32[2,8,2,32,1024]{4,3,2,1,0:T(8,128)S(1)} custom-call(f32[32,1024]{1,0:T(8,128)S(1)} %pad_maximum_fusion.w_ref), custom_call_target="tpu_custom_call" | custom-call | flops 1000000 | bytes 4194304 | tf_op jit(solution)/shard_map/pallas_call | solution.py:53
  51.9 0.0 copy-start.1
  51.9 1.9 %copy-done.1 = f32[2,8,2,32,1024]{4,3,2,1,0:T(8,128)} copy-done((f32[2,8,2,32,1024]{4,3,2,1,0:T(8,128)}, f32[2,8,2,32,1024]{4,3,2,1,0:T(8,128)S(1)}, u32[]{:S(2)}) %copy-start.1) | copy-done | bytes 4194328
  53.8 0.0 copy-done.3
  53.8 1.3 fusion
  55.2 1.3 fusion.2
  56.5 1.3 convolution_bitcast_fusion.1
  57.8 1.3 convolution_bitcast_fusion.2
  59.1 0.1 broadcast_bitcast_fusion
  59.2 0.0 copy-done
  59.2 0.0 copy-start.5
  59.2 7.1 %convolution_bitcast_fusion.p_ref = f32[512,1024]{1,0:T(8,128)} fusion(f32[1024,1024]{1,0:T(8,128)} %bitcast.17, f32[1024,512]{1,0:T(8,128)S(1)} %copy-done), kind=kOutput, calls=%fused_computation | convolution fusion | flops 3221225472 | bytes 8388608 | tf_op jit(solution)/shard_map/dot_general | solution.py:14
  66.3 0.1 pad_dynamic-slice_fusion.4
  66.4 0.0 copy-done.4
  66.4 0.0 copy-done.5
  66.4 0.8 dynamic-slice_add_fusion
  67.2 0.0 collective-permute-done.u_ref
  67.2 1.6 %copy-done.2 = f32[512,1024]{1,0:T(8,128)S(1)} copy-done((f32[512,1024]{1,0:T(8,128)S(1)}, f32[512,1024]{1,0:T(8,128)}, u32[]{:S(2)}) %copy-start.2) | copy-done | bytes 2097176
  68.8 79.2 %shard_map.86 = (f32[32,1024]{1,0:T(8,128)S(1)}, f32[32,256]{1,0:T(8,128)S(1)}, f32[16,256]{1,0:T(8,128)S(1)}) custom-call(f32[512,1024]{1,0:T(8,128)S(1)} %copy-done.2, f32[32,1024]{1,0:T(8,128)S(1)} %collective-permute-done.u_ref, f32[48,256]{1,0:T(8,128)S(1)} %pad_maximum_fusion.1.base_ref), custom_call_target="tpu_custom_call" | custom-call | flops 1000000 | bytes 8388608 | tf_op jit(solution)/shard_map/pallas_call | solution.py:53
  148.1 0.7 broadcast_multiply_fusion
  148.7 0.6 copy.15
  149.3 0.6 copy.16
  (10 shorter events, 0.1 us)
Async XLA Ops:
  0.6 58.6 %copy-start = (f32[1024,512]{1,0:T(8,128)S(1)}, f32[1024,512]{1,0:T(8,128)}, u32[]{:S(2)}) copy-start(f32[1024,512]{1,0:T(8,128)} %param.6) | copy-start | bytes 6291460
  5.9 47.9 %copy-start.3 = (f32[512,256]{1,0:T(8,128)S(1)}, f32[512,256]{1,0:T(8,128)}, u32[]{:S(2)}) copy-start(f32[512,256]{1,0:T(8,128)} %param.9) | copy-start | bytes 1572868
  5.9 61.3 %collective-permute-start = (f32[32,1024]{1,0:T(8,128)S(1)}, f32[32,1024]{1,0:T(8,128)S(1)}, u32[]{:S(2)}, u32[]{:S(2)}) collective-permute-start(f32[32,1024]{1,0:T(8,128)S(1)} %pad_maximum_fusion.w_ref), channel_id=1, source_target_pairs={{0,0},{1,32},{2,64},{3,96},{4,128},{5,160},{6,192},{7,224},{8,256}... | collective-permute-start | bytes 393224 | tf_op jit(solution)/shard_map/ppermute | solution.py:261
  51.9 1.9 %copy-start.1 = (f32[2,8,2,32,1024]{4,3,2,1,0:T(8,128)}, f32[2,8,2,32,1024]{4,3,2,1,0:T(8,128)S(1)}, u32[]{:S(2)}) copy-start(f32[2,8,2,32,1024]{4,3,2,1,0:T(8,128)S(1)} %shard_map.85) | copy-start | bytes 12582916
  59.2 7.2 %copy-start.4 = (f32[256,256]{1,0:T(8,128)S(1)}, f32[256,256]{1,0:T(8,128)}, u32[]{:S(2)}) copy-start(f32[256,256]{1,0:T(8,128)} %convolution_bitcast_fusion.1) | copy-start | bytes 786436
  59.2 7.2 %copy-start.5 = (f32[256,256]{1,0:T(8,128)S(1)}, f32[256,256]{1,0:T(8,128)}, u32[]{:S(2)}) copy-start(f32[256,256]{1,0:T(8,128)} %convolution_bitcast_fusion.2) | copy-start | bytes 786436
  67.2 1.6 %copy-start.2 = (f32[512,1024]{1,0:T(8,128)S(1)}, f32[512,1024]{1,0:T(8,128)}, u32[]{:S(2)}) copy-start(f32[512,1024]{1,0:T(8,128)} %convolution_bitcast_fusion.p_ref) | copy-start | bytes 6291460

commit v5 on v4

--- a/solution.py
+++ b/solution.py
@@ -58,7 +58,7 @@
         scratch_shapes=scratch,
         cost_estimate=pl.CostEstimate(flops=1000000, bytes_accessed=sent, transcendentals=0),
         compiler_params=pltpu.CompilerParams(
-            collective_id=collective_id, has_side_effects=True, vmem_limit_bytes=40 * 2**20
+            collective_id=collective_id, has_side_effects=True, vmem_limit_bytes=18 * 2**20
         ),
     )(*operands)
 
@@ -259,18 +259,19 @@
     w = jnp.concatenate([u[:, : 2 * W], x[0], x[1]], axis=1)
     moves = [(q, (q % 16) * 32 + q // 16) for q in range(512)]
     w_own = lax.ppermute(w, ("grp", "blk"), moves)
+    def rows_of(a, first, count):
+        return lax.dynamic_slice_in_dim(a, first, count, 0)
+
+    pair = rows_of(diag_inv, blk * 16, 16)
+    base_parent = dot(pair, rows_of(scaled_parent_panel, (blk // 16) * W, W), 1, 0, HIGHEST)
+    lower = jnp.maximum(blk - 16, 0)
+    v_low = rows_of(scaled_parent_panel, (lower // 8) * W, W)
+    v_some = lax.dynamic_slice_in_dim(v_low, (lower % 8) * 32, 32, 1)
+    left = dot(v_some, rows_of(diag_inv, (lower // 8) * W, W), 0, 0, HIGHEST)
+    base_low = jnp.where(blk >= 16, dot(left, v_low, 1, 0, HIGHEST), 0.0)
+    base = jnp.concatenate([rows_of(diag_inv, blk * 32, 32) + base_low, base_parent], axis=0)
+    w, base = lax.optimization_barrier((w, base))
     gathered = gather_rows(w)
-    base_parent = [dot(diag_inv[c * W : (c + 1) * W], v[c], 1, 0, HIGHEST) for c in (0, 1)]
-    base_low = [dot(v[c], base_parent[c], 0, 0, HIGHEST) for c in (0, 1)]
-    zero = jnp.zeros((2 * W, W), jnp.float32)
-    base_diag = diag_inv + jnp.concatenate([zero] + base_low, axis=0)
-    base = jnp.concatenate(
-        [
-            lax.dynamic_slice_in_dim(base_diag, blk * 32, 32, 0),
-            lax.dynamic_slice_in_dim(jnp.concatenate(base_parent, axis=0), blk * 16, 16, 0),
-        ],
-        axis=0,
-    )
     partial = dot(sigma_anc, gathered, 0, 0)
     t, cov_diag, cov_parent = scatter_and_sum(partial, w_own, base)
     own = listed(struct_upper, struct_lower, (blk * 16 + grp) // 8)

time: 150 us -> 137 us (0.913)
  matrix products: 14.6 us -> 9.51 us
  local copies, waits for them, and re-layouts: 4.98 us -> 1.39 us
  Pallas kernels: 119 us -> 116 us
    dot_general x7 -> x6, matrix products: 14.6 us -> 9.51 us  [dot(): lax.dot_general(a, b, (((ca,), (cb,)), ((), ())), precision=precision, pr...]
    unnamed x18 -> x10, local copies, waits for them, and re-layouts: 4.9 us -> 1.39 us
    pallas_call x2, Pallas kernels: 119 us -> 116 us  [call(): pl.pallas_call(kernel, out_shape=[jax.ShapeDtypeStruct(shape, jnp.float32...]
  transfers between devices with their start and end apart: 1 -> 1, of which waited for: 0 -> 0; matrix products, arithmetic and copies ran while one was open for 9% -> 5% of each run, Pallas kernels for 27% -> 27%
where the time goes in v5:
time: 137 us
  Pallas kernels  116 us (85%)
  matrix products  9.51 us (7%)
  starting transfers between devices  6.03 us (4%)
  other arithmetic  3.53 us (3%)
  local copies, waits for them, and re-layouts  1.39 us (1%)
    pallas_call x2, Pallas kernels, call(): pl.pallas_call(kernel, out_shape=[jax.ShapeDtypeStruct(shape, jnp.float32...  116 us
    dot_general x6, matrix products, dot(): lax.dot_general(a, b, (((ca,), (cb,)), ((), ())), precision=precision, pr...  9.51 us
    ppermute x1, starting transfers between devices, per_device(): w_own = lax.ppermute(w, ('grp', 'blk'), moves)  6.03 us
  transfers between devices with their start and end apart: 1, of which 0 were waited for; matrix products, arithmetic and copies ran while one was open for 5% of the time, Pallas kernels for 27%

profile of v5, /device:TPU:1, one launch (start us, length us, event | category | flops | bytes accessed | tf_op | source)
XLA Modules:
  0.0 137.0 jit_solution(14990658043794220839)
XLA Ops:
  0.6 0.0 copy-start
  0.6 0.0 copy-start.1
  0.7 1.0 compare_reduce_fusion.1
  1.7 0.8 compare_reduce_fusion
  2.5 0.1 add_convert_fusion
  2.6 0.1 broadcast_bitcast_fusion.1
  2.7 0.9 broadcast_multiply_fusion.1
  3.6 1.2 convolution_subtract_fusion
  4.8 1.2 convolution_subtract_fusion.1
  6.0 6.0 %collective-permute-start = (f32[32,1024]{1,0:T(8,128)S(1)}, f32[32,1024]{1,0:T(8,128)S(1)}, u32[]{:S(2)}, u32[]{:S(2)}) collective-permute-start(f32[32,1024]{1,0:T(8,128)S(1)} %pad_maximum_fusion.w_ref), channel_id=1, source_target_pairs={{0,0},{1,32},{2,64},{3,96},{4,128},{5,160},{6,192},{7,224},{8,256}... | collective-permute-start | bytes 393224 | tf_op jit(solution)/shard_map/ppermute | solution.py:261
  12.0 1.2 fusion.1
  13.2 1.5 %fusion.4 = f32[32,256]{1,0:T(8,128)S(1)} fusion(f32[1024,256]{1,0:T(8,128)} %param.8, s32[]{:T(128)S(6)} %select_n.68, f32[512,256]{1,0:T(8,128)} %param.9, s32[]{:T(128)S(6)} %select_n.64, s32[]{:T(128)S(6)} %select_n.67), kind=kOutput, calls=%fused_computation.8 | convolution fusion | flops 25165824 | bytes 425996 | tf_op jit(solution)/shard_map/dot_general | solution.py:14
  14.7 0.0 copy-done.1
  14.7 1.0 fusion
  15.8 36.7 %shard_map.85 = f32[2,8,2,32,1024]{4,3,2,1,0:T(8,128)S(1)} custom-call(f32[32,1024]{1,0:T(8,128)S(1)} %pad_maximum_fusion.w_ref), custom_call_target="tpu_custom_call" | custom-call | flops 1000000 | bytes 4194304 | tf_op jit(solution)/shard_map/pallas_call | solution.py:53
  52.5 0.1 broadcast_bitcast_fusion
  52.6 0.0 copy-done
  52.6 3.5 %convolution_bitcast_fusion.p_ref = f32[512,1024]{1,0:T(8,128)S(1)} fusion(f32[1024,1024]{1,0:T(8,128)S(1)} %bitcast.12, f32[1024,512]{1,0:T(8,128)S(1)} %copy-done), kind=kOutput, calls=%fused_computation | convolution fusion | flops 3221225472 | bytes 8388608 | tf_op jit(solution)/shard_map/dot_general | solution.py:14
  56.1 0.0 collective-permute-done.u_ref
  56.1 78.9 %shard_map.86 = (f32[32,1024]{1,0:T(8,128)S(1)}, f32[32,256]{1,0:T(8,128)S(1)}, f32[16,256]{1,0:T(8,128)S(1)}) custom-call(f32[512,1024]{1,0:T(8,128)S(1)} %convolution_bitcast_fusion.p_ref, f32[32,1024]{1,0:T(8,128)S(1)} %collective-permute-done.u_ref, f32[48,256]{1,0:T(8,128)S(1)} %pad_maximum_fusion.1.base_ref), custom_call_target="tpu_custom_call" | custom-call | flops 1000000 | bytes 8388608 | tf_op jit(solution)/shard_map/pallas_call | solution.py:53
  135.1 0.7 broadcast_multiply_fusion
  135.7 0.6 copy.15
  136.4 0.6 copy.16
  (6 shorter events, 0.0 us)
Async XLA Ops:
  0.6 51.9 %copy-start = (f32[1024,512]{1,0:T(8,128)S(1)}, f32[1024,512]{1,0:T(8,128)}, u32[]{:S(2)}) copy-start(f32[1024,512]{1,0:T(8,128)} %param.6) | copy-start | bytes 6291460
  0.6 14.1 %copy-start.1 = (f32[512,256]{1,0:T(8,128)S(1)}, f32[512,256]{1,0:T(8,128)}, u32[]{:S(2)}) copy-start(f32[512,256]{1,0:T(8,128)} %param.9) | copy-start | bytes 1572868
  6.0 50.2 %collective-permute-start = (f32[32,1024]{1,0:T(8,128)S(1)}, f32[32,1024]{1,0:T(8,128)S(1)}, u32[]{:S(2)}, u32[]{:S(2)}) collective-permute-start(f32[32,1024]{1,0:T(8,128)S(1)} %pad_maximum_fusion.w_ref), channel_id=1, source_target_pairs={{0,0},{1,32},{2,64},{3,96},{4,128},{5,160},{6,192},{7,224},{8,256}... | collective-permute-start | bytes 393224 | tf_op jit(solution)/shard_map/ppermute | solution.py:261
